TPU v7x, 128 devices: a whole 4x4x4 slice. The times are simulated.
128 devices in a mesh: tm: 8 (over x, core), ctx: 16 (over y, z).
Axes of the slice: x: 4, y: 4, z: 4, core: 2. Of those that a mesh axis runs over, the one named last changes fastest.
Arguments:
- iterate: float32 [8, 2688, 1536], P('tm', 'ctx'), may hold values from -6 to 6
- anchor: float32 [2688, 1536], P('ctx'), may hold values from -6 to 6
- frame_index: int32 [2688], P('ctx'), may hold values from 0 to 15, never falling along the last dimension, each value on 1 to 336 neighbouring positions
- noise_steps: int32 [8, 16], P('tm'), may hold values from 0 to 11
- qkv_weight: bfloat16 [1536, 4608], replicated, may hold values from -0.15625 to 0.15625
- out_weight: bfloat16 [1536, 1536], replicated, may hold values from -0.15625 to 0.15625
- mod_weight: bfloat16 [256, 4608], replicated, may hold values from -0.375 to 0.375
Outputs:
- updated: float32 [8, 2688, 1536], P('tm', 'ctx')
Inputs may be any that keep to these rules, and one draw needn't show every extreme that they name: `frame_index`: frame numbers never fall along the sequence; each of the 16 frames holds 1 to 336 tokens.
All inputs are finite; a program needn't handle non-finite values.
Results may differ from a plain program's by a relative error of at most 0.00051.
Values may be sent and summed in bfloat16 or wider, within the bound.
No kernel may reach another device: no remote copies, remote signals or barrier semaphores. Data moves between devices by JAX's collectives and lax.ppermute only.
A program may use at most 192 MiB of HBM per device.

v0:
```python
import math
import jax
import jax.numpy as jnp
from jax import lax
from jax.sharding import PartitionSpec as P

HD = 128
NSCHED = 12
shift_factor = 5.0
norm_eps = 1e-06


def carried_in(part, axis, combine, identity):
    place = lax.axis_index(axis)
    gathered = lax.all_gather(part, axis)
    state = jnp.zeros_like(part) + jnp.asarray(identity, part.dtype)

    def one(turn, state):
        return combine(state, lax.dynamic_index_in_dim(gathered, turn, 0, False))

    return lax.fori_loop(0, place, one, state)


def noise_level(level_index):
    fraction = level_index / NSCHED
    return shift_factor * fraction / (1.0 + (shift_factor - 1.0) * fraction)


def frame_terms(steps_row, mod_weight):
    level_float = steps_row.astype(jnp.float32)
    upper = noise_level(level_float + 1.0)
    lower = noise_level(level_float)
    step_size = upper - lower
    half_freq = mod_weight.shape[0] // 2
    rates = jnp.exp(-math.log(10000.0) * jnp.arange(half_freq, dtype=jnp.float32) / half_freq)
    angles = (1000.0 * upper)[:, None] * rates[None, :]
    features = jnp.concatenate([jnp.cos(angles), jnp.sin(angles)], axis=1).astype(jnp.bfloat16)
    modulation = jnp.dot(features, mod_weight, preferred_element_type=jnp.float32)
    return (modulation, step_size)


def layer_norm(latent):
    center = latent - jnp.mean(latent, axis=-1, keepdims=True)
    spread = jnp.mean(center * center, axis=-1, keepdims=True)
    return center * lax.rsqrt(spread + norm_eps)


def head_norm(projected):
    tok_rows = projected.shape[0]
    model_width = projected.shape[1]
    split = projected.reshape(tok_rows, model_width // HD, HD)
    scaled = split * lax.rsqrt(jnp.mean(split * split, axis=-1, keepdims=True) + norm_eps)
    return scaled.reshape(tok_rows, model_width).astype(jnp.bfloat16)


def attend(query_heads, key_rows, value_rows, frame_piece, frame_index):
    piece_rows = key_rows.shape[0]
    head_count = query_heads.shape[1]
    key_heads = key_rows.reshape(piece_rows, head_count, HD)
    value_heads = value_rows.reshape(piece_rows, head_count, HD)
    scores = jnp.einsum(
        "qhd,khd->hqk", query_heads, key_heads, preferred_element_type=jnp.float32
    ) * HD ** (-0.5)
    allowed = frame_piece[None, :] <= frame_index[:, None]
    weights = jnp.where(allowed[None, :, :], jnp.exp(scores), 0.0)
    numerator = jnp.einsum(
        "hqk,khd->hqd",
        weights.astype(jnp.bfloat16),
        value_heads,
        preferred_element_type=jnp.float32,
    )
    denominator = jnp.sum(weights, axis=-1)
    return (numerator, denominator)


def velocity_drift(latent, steps_row, frame_index, qkv_weight, out_weight, mod_weight):
    tok_rows = latent.shape[0]
    model_width = latent.shape[1]
    head_count = model_width // HD
    frame_count = steps_row.shape[0]
    modulation, step_size = frame_terms(steps_row, mod_weight)
    one_hot = (frame_index[:, None] == jnp.arange(frame_count, dtype=jnp.int32)[None, :]).astype(
        jnp.float32
    )
    tok_mod = jnp.dot(one_hot, modulation, precision=lax.Precision.HIGHEST)
    tok_step = jnp.dot(one_hot, step_size[:, None], precision=lax.Precision.HIGHEST)[:, 0]
    shift_part = tok_mod[:, :model_width]
    scale_part = tok_mod[:, model_width : 2 * model_width]
    gate_part = tok_mod[:, 2 * model_width :]
    normed = (layer_norm(latent) * (1.0 + scale_part) + shift_part).astype(jnp.bfloat16)
    projected = jnp.dot(normed, qkv_weight, preferred_element_type=jnp.float32)
    queries = head_norm(projected[:, :model_width])
    key_rows = head_norm(projected[:, model_width : 2 * model_width])
    values = projected[:, 2 * model_width :].astype(jnp.bfloat16)
    query_heads = queries.reshape(tok_rows, head_count, HD)
    numerator, denominator = attend(
        query_heads,
        lax.all_gather(key_rows, "ctx", axis=0, tiled=True),
        lax.all_gather(values, "ctx", axis=0, tiled=True),
        lax.all_gather(frame_index, "ctx", axis=0, tiled=True),
        frame_index,
    )
    attended = (numerator / denominator[:, :, None]).astype(jnp.bfloat16)
    attended = attended.transpose(1, 0, 2).reshape(tok_rows, model_width)
    branch = jnp.dot(attended, out_weight, preferred_element_type=jnp.float32)
    return -tok_step[:, None] * (latent + gate_part * branch)


def add_terms(earlier, later):
    return earlier + later


def per_device(iterate, anchor, frame_index, noise_steps, qkv_weight, out_weight, mod_weight):
    position = 0
    drifts = [
        velocity_drift(
            iterate[position],
            noise_steps[position],
            frame_index,
            qkv_weight,
            out_weight,
            mod_weight,
        )
    ]
    block_total = drifts[0]
    earlier = carried_in(block_total, "tm", add_terms, jnp.zeros_like(block_total))
    running = earlier
    position = 0
    running = running + drifts[position]
    results = [anchor + running]
    return jnp.stack(results, axis=0)


def solution(mesh):
    placed = (P("tm", "ctx", None), P("ctx", None), P("ctx"), P("tm", None), P(), P(), P())
    return jax.shard_map(
        per_device, mesh=mesh, in_specs=placed, out_specs=P("tm", "ctx", None), check_vma=False
    )
```

profile of v0, /device:TPU:15, one launch (start us, length us, event | category | flops | bytes accessed | tf_op | source)
XLA Modules:
  0.0 275.0 jit_solution(8744244046365026407)
XLA Ops:
  6.6 0.8 multiply_bitcast_fusion
  7.4 1.6 reduce_sum.45
  8.9 1.5 multiply_reduce_fusion
  10.4 0.1 fusion.36
  10.5 0.4 fusion.38
  11.0 2.1 fusion.32
  13.1 8.9 %fusion.21 = f32[168,4608]{1,0:T(8,128)S(1)} fusion(bf16[1536,4608]{1,0:T(8,128)(2,1)} %param.13, f32[168,4608]{1,0:T(8,128)S(1)} %fusion.32, f32[1,168,1536]{2,1,0:T(8,128)S(1)} %copy-done.2, f32[168]{0:T(256)S(1)} %add_rsqrt_fusion.2, f32[168]{0:T(256)S(1)} %broadcast_multiply_fusion), kind=kOutput, calls=%fused_computation.29 | convolution fusion | flops 2379718656 | bytes 20350976 | tf_op jit(solution)/shard_map/dot_general | solution.py:91
  22.0 1.7 copy-done.3
  23.8 1.4 slice_multiply_fusion.1
  25.2 1.4 mul.143
  26.7 0.4 reduce_sum.47
  27.1 0.1 copy.25
  27.2 0.1 copy.26
  27.3 1.4 mul.148
  28.8 0.4 reduce_sum.48
  29.2 0.1 copy.27
  29.3 0.1 copy.28
  29.4 0.4 mul.144
  29.8 0.4 mul.149
  30.2 3.2 %fusion.23 = (bf16[21,12,8,128]{3,2,1,0:T(8,128)(2,1)S(1)}, bf16[168,1536]{1,0:T(8,128)(2,1)}) fusion(f32[21,8,12,128]{3,2,1,0:T(8,128)S(1)} %bitcast.64, f32[168,4608]{1,0:T(8,128)} %copy-done.3, f32[21,8,12,128]{3,2,1,0:T(8,128)S(1)} %bitcast.65), kind=kLoop, calls=%fused_computation.30 | loop fusion | flops 1032192 | bytes 5160960
  33.5 0.0 all-gather.7.cloned.1.call-start
  33.6 2.1 slice.49
  35.6 0.0 all-gather.7.cloned.1.call-update
  35.6 0.0 all-gather.9.cloned.1.call-start
  35.7 0.2 fusion.33
  35.9 0.0 copy-done.7
  36.0 0.7 dynamic-slice
  37.3 0.3 dynamic-update-slice
  37.6 59.2 %all-reduce = s32[2688]{0:T(1024)S(1)} all-reduce(s32[2688]{0:T(1024)S(1)} %dynamic-update-slice), channel_id=1, replica_groups=mesh['tm'=8,'ctx'=16] {'ctx'}, use_global_device_ids=true, to_apply=%add | all-reduce | flops 2688 | bytes 21504
  96.7 0.3 broadcast_compare_fusion
  97.1 9.8 %all-gather.5.cloned.1.call-done = bf16[2688,1536]{1,0:T(8,128)(2,1)} async-done(((bf16[168,1536]{1,0:T(8,128)(2,1)}), bf16[2688,1536]{1,0:T(8,128)(2,1)}) %all-gather.5.cloned.1.call-update) | async-done | bytes 8257552 | tf_op jit(solution)/shard_map/all_gather | solution.py:98
  106.9 11.2 %copy.29 = bf16[2688,1536]{0,1:T(8,128)(2,1)} copy(bf16[2688,1536]{1,0:T(8,128)(2,1)} %all-gather.5.cloned.1.call-done) | data formatting | bytes 16515072 | tf_op jit(solution)/shard_map/all_gather | solution.py:98
  118.1 12.6 %fusion = (f32[12,168]{1,0:T(8,128)S(1)}, f32[12,168,2688]{2,1,0:T(8,128)}) fusion(pred[168,2688]{1,0:T(8,128)(4,1)S(1)} %broadcast_compare_fusion, bf16[2688,12,128]{0,2,1:T(8,128)(2,1)} %bitcast.62, bf16[21,12,8,128]{3,2,1,0:T(8,128)(2,1)S(1)} %get-tuple-element.39), kind=kOutput, calls=%fused_computation.2 | convolution fusion | flops 1403521024 | bytes 30909312 | tf_op jit(solution)/shard_map/qhd,khd->hqk/dot_general | solution.py:61
  130.7 48.2 %all-gather.7.cloned.1.call-done = bf16[2688,1536]{1,0:T(8,128)(2,1)} async-done(((bf16[168,1536]{1,0:T(8,128)(2,1)}), bf16[2688,1536]{1,0:T(8,128)(2,1)}) %all-gather.7.cloned.1.call-update) | async-done | bytes 8257552 | tf_op jit(solution)/shard_map/all_gather | solution.py:99
  178.9 11.2 %copy.32 = bf16[2688,1536]{0,1:T(8,128)(2,1)} copy(bf16[2688,1536]{1,0:T(8,128)(2,1)} %all-gather.7.cloned.1.call-done) | data formatting | bytes 16515072 | tf_op jit(solution)/shard_map/all_gather | solution.py:99
  190.1 12.5 %fusion.18 = bf16[12,21,8,128]{3,2,1,0:T(8,128)(2,1)S(1)} fusion(bf16[2688,12,128]{0,2,1:T(8,128)(2,1)} %bitcast.63, f32[12,168,2688]{2,1,0:T(8,128)} %get-tuple-element.46, pred[168,2688]{1,0:T(8,128)(4,1)S(1)} %broadcast_compare_fusion, f32[168,12]{0,1:T(8,128)S(1)} %bitcast.68), kind=kOutput, calls=%fused_computation.27 | convolution fusion | flops 1404039168 | bytes 30909312 | tf_op jit(solution)/shard_map/hqk,khd->hqd/dot_general | solution.py:66
  202.6 4.6 %fusion.8 = f32[168,1536]{1,0:T(8,128)} fusion(bf16[1536,1536]{1,0:T(8,128)(2,1)} %param.14, f32[168,4608]{1,0:T(8,128)} %copy-done.4, f32[1,168,1536]{2,1,0:T(8,128)S(1)} %copy-done.2, bf16[12,21,8,128]{3,2,1,0:T(8,128)(2,1)S(1)} %fusion.18, f32[168]{0:T(256)S(1)} %neg.4), kind=kOutput, calls=%fused_computation.10 | convolution fusion | flops 793497600 | bytes 8331936 | tf_op jit(solution)/shard_map/dot_general | solution.py:105
  207.3 47.7 %all-gather.9.cloned.1.call-done = f32[1344,1536]{1,0:T(8,128)} async-done(((f32[168,1536]{1,0:T(8,128)}), f32[1344,1536]{1,0:T(8,128)}) %all-gather.9.cloned.1.call-update) | async-done | bytes 8257552 | tf_op jit(solution)/shard_map/all_gather | solution.py:15
  254.9 0.1 broadcast_in_dim.10
  255.0 10.8 %while.10 = (s32[]{:T(128)}, f32[168,1536]{1,0:T(8,128)S(1)}, s32[]{:T(128)}, f32[8,168,1536]{2,1,0:T(8,128)}, s32[]{:T(128)}, /*index=5*/s32[]{:T(128)}, s32[]{:T(128)}) while((s32[]{:T(128)}, f32[168,1536]{1,0:T(8,128)S(1)}, s32[]{:T(128)}, f32[8,168,1536]{2,1,0:T(8,128)}, s32[]{:T(128)}, /*index=5*/s32[]{:T(128)}, s32[]{:T(128)}) %tuple.32), condition=%wide.region_6.7_spmd, body=%wide.region_5.6_spmd.sunk | while | flops 258053 | bytes 3096691 | solution.py:21
  255.1 1.6 bitcast_add_fusion.2
  256.7 1.5 bitcast_add_fusion.2
  258.2 1.5 bitcast_add_fusion.2
  259.8 1.5 bitcast_add_fusion.2
  261.3 1.5 bitcast_add_fusion.2
  262.8 1.5 bitcast_add_fusion.2
  264.3 1.5 bitcast_add_fusion.2
  265.8 2.7 add_bitcast_fusion
  (24 shorter events, 0.1 us)
Async XLA Ops:
  6.5 4.0 %copy-start = (bf16[256,4608]{1,0:T(8,128)(2,1)S(1)}, bf16[256,4608]{1,0:T(8,128)(2,1)}, u32[]{:S(2)}) copy-start(bf16[256,4608]{1,0:T(8,128)(2,1)} %param.15) | copy-start | bytes 7077892
  6.5 6.5 %copy-start.2 = (f32[1,168,1536]{2,1,0:T(8,128)S(1)}, f32[1,168,1536]{2,1,0:T(8,128)}, u32[]{:S(2)}) copy-start(f32[1,168,1536]{2,1,0:T(8,128)} %param.9) | copy-start | bytes 3096580
  6.5 100.4 %all-gather.5.cloned.1.call-start = ((), (), s32[]{:S(2)}) async-start(), calls=%async_computation | async-start | bytes 8773632 | tf_op jit(solution)/shard_map/all_gather | solution.py:98
  13.1 8.9 %copy-start.4 = (f32[168,4608]{1,0:T(8,128)}, f32[168,4608]{1,0:T(8,128)S(1)}, u32[]{:S(2)}) copy-start(f32[168,4608]{1,0:T(8,128)S(1)} %fusion.32) | copy-start | bytes 9289732
  22.0 1.8 copy-start.3
  26.6 9.1 %copy-start.5 = (s32[168]{0:T(256)S(1)}, s32[168]{0:T(256)}, u32[]{:S(2)}) copy-start(s32[168]{0:T(256)} %param.11) | copy-start | bytes 2020
  26.6 9.1 %copy-start.6 = (s32[1,16]{1,0:T(1,128)S(1)}, s32[1,16]{1,0:T(1,128)}, u32[]{:S(2)}) copy-start(s32[1,16]{1,0:T(1,128)} %param.12) | copy-start | bytes 196
  26.7 9.3 %copy-start.7 = (u32[128]{0:T(128)S(1)}, u32[128]{0:T(128)}, u32[]{:S(2)}) copy-start(u32[128]{0:T(128)} %constant.59) | copy-start | bytes 1540
  33.5 145.4 %all-gather.7.cloned.1.call-start = ((), (), s32[]{:S(2)}) async-start(), calls=%async_computation.1 | async-start | bytes 8773632 | tf_op jit(solution)/shard_map/all_gather | solution.py:99
  35.6 219.3 %all-gather.9.cloned.1.call-start = ((), (), s32[]{:S(2)}) async-start(), calls=%async_computation.2 | async-start | bytes 9289728 | tf_op jit(solution)/shard_map/all_gather | solution.py:15
  255.0 13.5 %copy-start.1 = (bf16[256,4608]{1,0:T(8,128)(2,1)S(1)}, bf16[256,4608]{1,0:T(8,128)(2,1)}, u32[]{:S(2)}) copy-start(bf16[256,4608]{1,0:T(8,128)(2,1)} %param.15) | copy-start | bytes 7077892
Sparse Core Ops, SparseCore 0:
  33.6 73.2 all-gather.4
  109.1 69.7 all-gather.6
  207.4 47.4 all-gather.8
where the time goes:
time: 276 us; the launch traced here: 275 us
  waiting for transfers between devices  106 us (38%)
  blocking collectives  59.2 us (21%)
  matrix products  41.3 us (15%)
  local copies, waits for them, and re-layouts  31.3 us (11%)
  other arithmetic  23.1 us (8%)
  between operations  14 us (5%)
    unnamed x1, blocking collectives  59.2 us
    all_gather x1, waiting for transfers between devices, velocity_drift(): lax.all_gather(values, 'ctx', axis=0, tiled=True)  48.2 us
    all_gather x1, waiting for transfers between devices, carried_in(): gathered = lax.all_gather(part, axis)  47.7 us
    dot_general x1, matrix products, attend(): jnp.einsum('qhd,khd->hqk', query_heads, key_heads, preferred_element_type...  12.6 us
    dot_general x1, matrix products, attend(): jnp.einsum('hqk,khd->hqd', weights.astype(jnp.bfloat16), value_heads, pre...  12.5 us
    all_gather x1, local copies, waits for them, and re-layouts, velocity_drift(): lax.all_gather(key_rows, 'ctx', axis=0, tiled=True)  11.2 us
    all_gather x1, local copies, waits for them, and re-layouts, velocity_drift(): lax.all_gather(values, 'ctx', axis=0, tiled=True)  11.2 us
    add x7, other arithmetic, add_terms(): return earlier + later  10.6 us
  transfers between devices with their start and end apart: 3, of which 3 were waited for; matrix products, arithmetic and copies ran while one was open for 10% of the time, Pallas kernels for 0%

commit v1 on v0

--- a/solution.py
+++ b/solution.py
@@ -3,6 +3,7 @@
 import jax.numpy as jnp
 from jax import lax
 from jax.sharding import PartitionSpec as P
+from jax.lax import all_to_all, axis_size
 
 HD = 128
 NSCHED = 12
@@ -93,9 +94,12 @@
     key_rows = head_norm(projected[:, model_width : 2 * model_width])
     values = projected[:, 2 * model_width :].astype(jnp.bfloat16)
     query_heads = queries.reshape(tok_rows, head_count, HD)
+    views_plan = lambda w_in: jnp.concatenate(
+        all_to_all(jnp.stack(axis_size("ctx") * [w_in], axis=0), "ctx", 0, 0), axis=0
+    )
     numerator, denominator = attend(
         query_heads,
-        lax.all_gather(key_rows, "ctx", axis=0, tiled=True),
+        views_plan(key_rows),
         lax.all_gather(values, "ctx", axis=0, tiled=True),
         lax.all_gather(frame_index, "ctx", axis=0, tiled=True),
         frame_index,

time: 276 us -> 390 us (1.41)
  blocking collectives: 59.2 us -> 192 us
  waiting for transfers between devices: 106 us -> 65.7 us
  starting transfers between devices: 0.09 us -> 8.02 us
  local copies, waits for them, and re-layouts: 31.3 us -> 38.7 us
  matrix products: 41.3 us -> 45.2 us
    unnamed x1, blocking collectives: 59.2 us -> 192 us
    all_gather x1, waiting for transfers between devices: 48.2 us -> 0.01 us  [velocity_drift(): lax.all_gather(values, 'ctx', axis=0, tiled=True)]
    another operation x0 -> x2, local copies, waits for them, and re-layouts: none -> 19.4 us  [the longest x1 15.7 us: attend(): key_heads = key_rows.reshape(piece_rows, head_count, HD)]
    all_gather x1, waiting for transfers between devices: 47.7 us -> 65.6 us  [carried_in(): gathered = lax.all_gather(part, axis)]
    all_gather x1 -> x0, local copies, waits for them, and re-layouts: 11.2 us -> none  [velocity_drift(): lax.all_gather(key_rows, 'ctx', axis=0, tiled=True)]
    all_gather x1 -> x0, waiting for transfers between devices: 9.84 us -> none  [velocity_drift(): lax.all_gather(key_rows, 'ctx', axis=0, tiled=True)]
    all_to_all x0 -> x1, starting transfers between devices: none -> 7.98 us  [velocity_drift(): all_to_all(jnp.stack(axis_size('ctx') * [w_in], axis=0), 'ctx', 0, 0)]
  transfers between devices with their start and end apart: 3 -> 3, of which waited for: 3 -> 1; matrix products, arithmetic and copies ran while one was open for 10% -> 12% of each run, Pallas kernels for 0% -> 0%
where the time goes in v1:
time: 390 us; the launch traced here: 388 us
  blocking collectives  192 us (49%)
  waiting for transfers between devices  65.7 us (17%)
  matrix products  45.2 us (12%)
  local copies, waits for them, and re-layouts  38.7 us (10%)
  other arithmetic  24.7 us (6%)
  between operations  14.3 us (4%)
  starting transfers between devices  8.02 us (2%)
    unnamed x1, blocking collectives  192 us
    all_gather x1, waiting for transfers between devices, carried_in(): gathered = lax.all_gather(part, axis)  65.6 us
    dot_general x1, matrix products, attend(): jnp.einsum('qhd,khd->hqk', query_heads, key_heads, preferred_element_type...  16.5 us
    another operation x1, local copies, waits for them, and re-layouts, attend(): key_heads = key_rows.reshape(piece_rows, head_count, HD)  15.7 us
    dot_general x1, matrix products, attend(): jnp.einsum('hqk,khd->hqd', weights.astype(jnp.bfloat16), value_heads, pre...  12.5 us
    all_gather x1, local copies, waits for them, and re-layouts, velocity_drift(): lax.all_gather(values, 'ctx', axis=0, tiled=True)  11.7 us
    add x7, other arithmetic, add_terms(): return earlier + later  10.6 us
    dot_general x1, matrix products, velocity_drift(): projected = jnp.dot(normed, qkv_weight, preferred_element_type=jnp.float32)  8.91 us
  transfers between devices with their start and end apart: 3, of which 1 were waited for; matrix products, arithmetic and copies ran while one was open for 12% of the time, Pallas kernels for 0%

profile of v1, /device:TPU:15, one launch (start us, length us, event | category | flops | bytes accessed | tf_op | source)
XLA Modules:
  0.0 388.4 jit_solution(12093800887892175069)
XLA Ops:
  6.6 0.8 multiply_bitcast_fusion
  7.4 1.6 reduce_sum.45
  8.9 1.5 multiply_reduce_fusion
  10.4 0.1 fusion.37
  10.5 0.4 fusion.39
  11.0 2.1 fusion.33
  13.1 8.9 %fusion.23 = f32[168,4608]{1,0:T(8,128)S(1)} fusion(bf16[1536,4608]{1,0:T(8,128)(2,1)} %param.13, f32[168,4608]{1,0:T(8,128)S(1)} %fusion.33, f32[1,168,1536]{2,1,0:T(8,128)S(1)} %copy-done.2, f32[168]{0:T(256)S(1)} %add_rsqrt_fusion.2, f32[168]{0:T(256)S(1)} %broadcast_multiply_fusion), kind=kOutput, calls=%fused_computation.31 | convolution fusion | flops 2379718656 | bytes 20350976 | tf_op jit(solution)/shard_map/dot_general | solution.py:92
  22.0 1.6 copy-done.3
  23.6 0.8 slice.49
  24.5 0.0 all-gather.4.cloned.1.call-update
  24.5 3.0 slice_multiply_fusion.1
  27.5 1.4 mul.143
  28.9 0.4 reduce_sum.47
  29.4 0.1 copy.22
  29.5 0.1 copy.23
  29.6 1.4 mul.148
  31.0 0.4 reduce_sum.48
  31.4 0.1 copy.24
  31.5 0.1 copy.25
  31.7 0.4 mul.144
  32.1 0.4 mul.149
  32.5 3.2 fusion.25
  35.7 3.7 stack.4
  39.5 8.0 %all-to-all-start = ((bf16[16,168,1536]{2,1,0:T(8,128)(2,1)}), bf16[16,168,1536]{2,1,0:T(8,128)(2,1)}, u32[]{:S(2)}, u32[]{:S(2)}) async-start(bf16[16,168,1536]{2,1,0:T(8,128)(2,1)} %stack.4), calls=%async_computation | async-start | bytes 16515072 | tf_op jit(solution)/shard_map/all_to_all | solution.py:98
  47.4 0.0 all-gather.6.cloned.1.call-start
  47.5 0.2 fusion.34
  47.7 0.0 copy-done.8
  47.8 0.7 dynamic-slice
  49.1 0.3 dynamic-update-slice
  49.4 191.7 %all-reduce = s32[2688]{0:T(1024)S(1)} all-reduce(s32[2688]{0:T(1024)S(1)} %dynamic-update-slice), channel_id=1, replica_groups=mesh['tm'=8,'ctx'=16] {'ctx'}, use_global_device_ids=true, to_apply=%add | all-reduce | flops 2688 | bytes 21504
  241.1 0.3 broadcast_compare_fusion
  241.4 15.7 %reshape_reshape.3 = bf16[2688,12,128]{2,1,0:T(8,128)(2,1)} reshape(bf16[16,168,1536]{2,1,0:T(8,128)(2,1)} %all-to-all-done) | data formatting | bytes 16515072 | tf_op jit(solution)/shard_map/reshape;reshape | solution.py:60
  257.1 16.5 %fusion = (f32[12,168]{1,0:T(8,128)S(1)}, f32[12,168,2688]{2,1,0:T(8,128)}) fusion(pred[168,2688]{1,0:T(8,128)(4,1)S(1)} %broadcast_compare_fusion, bf16[2688,12,128]{2,1,0:T(8,128)(2,1)} %reshape_reshape.3, bf16[21,12,8,128]{3,2,1,0:T(8,128)(2,1)S(1)} %copy-done.5), kind=kOutput, calls=%fused_computation.2 | convolution fusion | flops 1403521024 | bytes 30909312 | tf_op jit(solution)/shard_map/qhd,khd->hqk/dot_general | solution.py:62
  273.5 11.7 %copy.28 = bf16[2688,1536]{0,1:T(8,128)(2,1)} copy(bf16[2688,1536]{1,0:T(8,128)(2,1)} %all-gather.4.cloned.1.call-done) | data formatting | bytes 16515072 | tf_op jit(solution)/shard_map/all_gather | solution.py:103
  285.2 12.5 %fusion.20 = bf16[12,21,8,128]{3,2,1,0:T(8,128)(2,1)S(1)} fusion(bf16[2688,12,128]{0,2,1:T(8,128)(2,1)} %bitcast.60, f32[12,168,2688]{2,1,0:T(8,128)} %get-tuple-element.46, pred[168,2688]{1,0:T(8,128)(4,1)S(1)} %broadcast_compare_fusion, f32[168,12]{0,1:T(8,128)S(1)} %bitcast.65), kind=kOutput, calls=%fused_computation.29 | convolution fusion | flops 1404039168 | bytes 30909312 | tf_op jit(solution)/shard_map/hqk,khd->hqd/dot_general | solution.py:67
  297.7 4.6 %fusion.10 = f32[168,1536]{1,0:T(8,128)} fusion(bf16[1536,1536]{1,0:T(8,128)(2,1)} %param.14, f32[168,4608]{1,0:T(8,128)} %copy-done.4, f32[1,168,1536]{2,1,0:T(8,128)S(1)} %copy-done.2, bf16[12,21,8,128]{3,2,1,0:T(8,128)(2,1)S(1)} %fusion.20, f32[168]{0:T(256)S(1)} %neg.4), kind=kOutput, calls=%fused_computation.12 | convolution fusion | flops 793497600 | bytes 8331936 | tf_op jit(solution)/shard_map/dot_general | solution.py:109
  302.3 0.0 all-gather.6.cloned.1.call-update
  302.3 65.6 %all-gather.6.cloned.1.call-done = f32[1344,1536]{1,0:T(8,128)} async-done(((f32[168,1536]{1,0:T(8,128)}), f32[1344,1536]{1,0:T(8,128)}) %all-gather.6.cloned.1.call-update) | async-done | bytes 8257552 | tf_op jit(solution)/shard_map/all_gather | solution.py:16
  368.0 0.1 broadcast_in_dim.10
  368.1 10.8 %while.10 = (s32[]{:T(128)}, f32[168,1536]{1,0:T(8,128)S(1)}, s32[]{:T(128)}, f32[8,168,1536]{2,1,0:T(8,128)}, s32[]{:T(128)}, /*index=5*/s32[]{:T(128)}, s32[]{:T(128)}) while((s32[]{:T(128)}, f32[168,1536]{1,0:T(8,128)S(1)}, s32[]{:T(128)}, f32[8,168,1536]{2,1,0:T(8,128)}, s32[]{:T(128)}, /*index=5*/s32[]{:T(128)}, s32[]{:T(128)}) %tuple.30), condition=%wide.region_6.7_spmd, body=%wide.region_5.6_spmd.sunk | while | flops 258053 | bytes 3096691 | solution.py:22
  368.1 1.6 bitcast_add_fusion.2
  369.8 1.5 bitcast_add_fusion.2
  371.3 1.5 bitcast_add_fusion.2
  372.8 1.5 bitcast_add_fusion.2
  374.3 1.5 bitcast_add_fusion.2
  375.8 1.5 bitcast_add_fusion.2
  377.3 1.5 bitcast_add_fusion.2
  378.8 2.7 add_bitcast_fusion
  (26 shorter events, 0.1 us)
Async XLA Ops:
  6.5 4.0 %copy-start = (bf16[256,4608]{1,0:T(8,128)(2,1)S(1)}, bf16[256,4608]{1,0:T(8,128)(2,1)}, u32[]{:S(2)}) copy-start(bf16[256,4608]{1,0:T(8,128)(2,1)} %param.15) | copy-start | bytes 7077892
  6.5 6.5 %copy-start.2 = (f32[1,168,1536]{2,1,0:T(8,128)S(1)}, f32[1,168,1536]{2,1,0:T(8,128)}, u32[]{:S(2)}) copy-start(f32[1,168,1536]{2,1,0:T(8,128)} %param.9) | copy-start | bytes 3096580
  6.5 267.0 %all-gather.4.cloned.1.call-start = ((), (), s32[]{:S(2)}) async-start(), calls=%async_computation.1 | async-start | bytes 8773632 | tf_op jit(solution)/shard_map/all_gather | solution.py:103
  13.1 8.9 %copy-start.4 = (f32[168,4608]{1,0:T(8,128)}, f32[168,4608]{1,0:T(8,128)S(1)}, u32[]{:S(2)}) copy-start(f32[168,4608]{1,0:T(8,128)S(1)} %fusion.33) | copy-start | bytes 9289732
  22.0 1.6 copy-start.3
  39.5 8.0 %copy-start.6 = (s32[168]{0:T(256)S(1)}, s32[168]{0:T(256)}, u32[]{:S(2)}) copy-start(s32[168]{0:T(256)} %param.11) | copy-start | bytes 2020
  39.5 8.0 %copy-start.7 = (s32[1,16]{1,0:T(1,128)S(1)}, s32[1,16]{1,0:T(1,128)}, u32[]{:S(2)}) copy-start(s32[1,16]{1,0:T(1,128)} %param.12) | copy-start | bytes 196
  39.5 8.3 %copy-start.8 = (u32[128]{0:T(128)S(1)}, u32[128]{0:T(128)}, u32[]{:S(2)}) copy-start(u32[128]{0:T(128)} %constant.59) | copy-start | bytes 1540
  39.5 201.9 %all-to-all-start = ((bf16[16,168,1536]{2,1,0:T(8,128)(2,1)}), bf16[16,168,1536]{2,1,0:T(8,128)(2,1)}, u32[]{:S(2)}, u32[]{:S(2)}) async-start(bf16[16,168,1536]{2,1,0:T(8,128)(2,1)} %stack.4), calls=%async_computation | async-start | bytes 16515072 | tf_op jit(solution)/shard_map/all_to_all | solution.py:98
  47.4 320.5 %all-gather.6.cloned.1.call-start = ((), (), s32[]{:S(2)}) async-start(), calls=%async_computation.2 | async-start | bytes 9289728 | tf_op jit(solution)/shard_map/all_gather | solution.py:16
  241.4 15.7 %copy-start.5 = (bf16[21,12,8,128]{3,2,1,0:T(8,128)(2,1)S(1)}, bf16[21,12,8,128]{3,2,1,0:T(8,128)(2,1)}, u32[]{:S(2)}) copy-start(bf16[21,12,8,128]{3,2,1,0:T(8,128)(2,1)} %get-tuple-element.39) | copy-start | bytes 1548292
  368.1 13.5 %copy-start.1 = (bf16[256,4608]{1,0:T(8,128)(2,1)S(1)}, bf16[256,4608]{1,0:T(8,128)(2,1)}, u32[]{:S(2)}) copy-start(bf16[256,4608]{1,0:T(8,128)(2,1)} %param.15) | copy-start | bytes 7077892
Sparse Core Ops, SparseCore 0:
  24.6 164.9 all-gather.3
  302.5 65.4 all-gather.5
